TPU v7x, 512 devices: a whole 4x8x8 slice. The times are simulated.
512 devices in a mesh: row: 16 (over y, core), col: 8 (over z), fib: 4 (over x).
Axes of the slice: x: 4, y: 8, z: 8, core: 2. Of those that a mesh axis runs over, the one named last changes fastest.
Arguments:
- values: bfloat16 [768, 12, 128, 128], P(('row', 'col'), 'fib'), may hold values from -3 to 3
- columns: int32 [768, 12], P(('row', 'col')), may hold values from 0 to 767, as said below
- counts: int32 [768], P(('row', 'col')), may hold values from 6 to 12, as said below
Outputs:
- square: bfloat16 [768, 12, 128, 128], P(('row', 'col'), 'fib')
- traces: float32 [2], replicated
Inputs may be any that keep to these rules, and one draw needn't show every extreme that they name: Slot 0 of block row i holds i. Every slot s >= 1 of row i, used or not, holds (i + o) mod 768 with 1 <= |o| <= 6, and the columns of one row are distinct. Row i uses slots 0 to counts[i] - 1; later slots are ignored. Some row uses all 12 slots.
All inputs are finite; a program needn't handle non-finite values.
Results may differ from a plain program's by a relative error of at most 0.001.
Values may be sent and summed in bfloat16 or wider, within the bound.
A program may use at most 128 MiB of HBM per device.

v0:
```python
import jax
import jax.numpy as jnp
from jax import lax
from jax.sharding import PartitionSpec as P

BAND = 6


def padded(array, sides, width):
    for axis, dim in sides:
        size, length = (lax.axis_size(axis), array.shape[dim])
        up = [(i, (i + 1) % size) for i in range(size)]
        down = [(j, i) for i, j in up]
        last = lax.slice_in_dim(array, length - width, length, axis=dim)
        initial = lax.slice_in_dim(array, 0, width, axis=dim)
        before = lax.ppermute(last, axis, up)
        after = lax.ppermute(initial, axis, down)
        array = jnp.concatenate([before, array, after], axis=dim)
    return array


def band_product(
    left_tiles, left_keep, fetch_index, target_cols, target_keep, window, window_cols, window_counts
):
    picked = jnp.take(window, fetch_index, axis=0)
    picked_cols = jnp.take(window_cols, fetch_index, axis=0)
    picked_counts = jnp.take(window_counts, fetch_index, axis=0)
    alive_slots = lax.broadcasted_iota(jnp.int32, picked_cols.shape, 1) < picked_counts[:, None]
    matches = (picked_cols[:, None, :] == target_cols[None, :, None]) & alive_slots[:, None, :]
    matches = matches & left_keep[:, None, None] & target_keep[None, :, None]
    chosen = jnp.einsum(
        "ajs,asxy->ajxy", matches.astype(jnp.bfloat16), picked, preferred_element_type=jnp.float32
    ).astype(jnp.bfloat16)
    return jnp.einsum("axy,ajyz->jxz", left_tiles, chosen, preferred_element_type=jnp.float32)


def body(values, columns, counts):
    rows_here = values.shape[0]
    share_count = values.shape[1]
    slot_count = columns.shape[1]
    block_total = rows_here * lax.axis_size(("row", "col"))
    fib_index = lax.axis_index("fib")
    full_rows = lax.all_gather(values, "fib", axis=1, tiled=True)
    window, window_cols, window_counts = (
        padded(full_rows, ((("row", "col"), 0),), BAND),
        padded(columns, ((("row", "col"), 0),), BAND),
        padded(counts, ((("row", "col"), 0),), BAND),
    )
    local_rows = jnp.arange(rows_here, dtype=jnp.int32)
    row_ids = lax.axis_index(("row", "col")) * rows_here + local_rows
    fetch_all = (columns - row_ids[:, None] + BAND) % block_total + local_rows[:, None]
    slot_ids = jnp.arange(slot_count, dtype=jnp.int32)
    keep_mask = slot_ids[None, :] < counts[:, None]
    first_slot = fib_index * share_count

    def one_row(operands):
        left_tiles, left_keep, fetch_index, target_cols, target_keep = operands
        return band_product(
            left_tiles,
            left_keep,
            fetch_index,
            target_cols,
            target_keep,
            window,
            window_cols,
            window_counts,
        )

    left_fetch = lax.dynamic_slice_in_dim(fetch_all, first_slot, share_count, 1)
    left_keep = lax.dynamic_slice_in_dim(keep_mask, first_slot, share_count, 1)
    partial_value = lax.map(one_row, (values, left_keep, left_fetch, columns, keep_mask))
    regrouped = lax.all_to_all(partial_value[None], "fib", split_axis=2, concat_axis=0, tiled=True)
    product = jnp.sum(regrouped, axis=0)
    is_first = (fib_index == 0).astype(jnp.float32)
    trace_values = is_first * jnp.sum(
        jnp.diagonal(values[:, 0].astype(jnp.float32), axis1=1, axis2=2)
    )
    trace_square = is_first * jnp.sum(jnp.diagonal(product[:, 0], axis1=1, axis2=2))
    traces = lax.psum(jnp.stack([trace_values, trace_square]), ("row", "col", "fib"))
    return (product.astype(jnp.bfloat16), traces)


def solution(mesh):
    in_specs = (P(("row", "col"), "fib", None, None), P(("row", "col"), None), P(("row", "col")))
    out_specs = (P(("row", "col"), "fib", None, None), P())
    return jax.shard_map(body, mesh=mesh, in_specs=in_specs, out_specs=out_specs, check_vma=False)
```

profile of v0, /device:TPU:1, one launch (start us, length us, event | category | flops | bytes accessed | tf_op | source)
XLA Modules:
  0.0 354.2 jit_solution(3832877042432415155)
XLA Ops:
  7.2 0.7 all-gather.2.cloned.1.call-update
  7.9 45.8 %all-gather.2.cloned.1.call-done = bf16[6,12,128,128]{3,2,1,0:T(8,128)(2,1)} async-done(((bf16[6,3,128,128]{3,2,1,0:T(8,128)(2,1)}), bf16[6,12,128,128]{3,2,1,0:T(8,128)(2,1)}) %all-gather.2.cloned.1.call-update) | async-done | bytes 2359312 | tf_op jit(solution)/shard_map/all_gather | solution.py:43
  53.7 3.3 collective-permute-start.4
  57.0 5.0 %collective-permute-start.5 = (bf16[6,12,128,128]{3,2,1,0:T(8,128)(2,1)}, bf16[6,12,128,128]{3,2,1,0:T(8,128)(2,1)}, u32[]{:S(2)}, u32[]{:S(2)}) collective-permute-start(bf16[6,12,128,128]{3,2,1,0:T(8,128)(2,1)} %all-gather.2.cloned.1.call-done), channel_id=1, source_target_pairs={{4,0},{8,4},{12,8},{16,12},{20,16},{24,20},{28,24},{32,28},{36,32}... | collective-permute-start | bytes 7077896 | tf_op jit(solution)/shard_map/ppermute | solution.py:17
  61.9 1.9 collective-permute-start
  63.8 4.9 %collective-permute-start.1 = (s32[6,12]{1,0:T(8,128)}, s32[6,12]{1,0:T(8,128)S(1)}, u32[]{:S(2)}, u32[]{:S(2)}) collective-permute-start(s32[6,12]{1,0:T(8,128)} %param.6), channel_id=1, source_target_pairs={{4,0},{8,4},{12,8},{16,12},{20,16},{24,20},{28,24},{32,28},{36,32}... | collective-permute-start | bytes 872 | tf_op jit(solution)/shard_map/ppermute | solution.py:17
  68.7 1.9 collective-permute-start.2
  70.7 0.7 iota_compare_fusion.1
  71.5 0.8 fusion.18
  72.3 39.8 %collective-permute-done.2 = s32[6]{0:T(128)S(1)} collective-permute-done((s32[6]{0:T(128)}, s32[6]{0:T(128)S(1)}, u32[]{:S(2)}, u32[]{:S(2)}) %collective-permute-start.2) | collective-permute-done | bytes 56 | tf_op jit(solution)/shard_map/ppermute | solution.py:16
  112.2 2.9 collective-permute-start.3
  115.1 1.5 collective-permute-done.3
  116.6 0.7 pad_add_fusion.1
  117.3 0.7 pad_add_fusion
  118.1 5.9 %pad_maximum_fusion = bf16[18,12,128,128]{3,2,1,0:T(8,128)(2,1)} fusion(bf16[6,12,128,128]{3,2,1,0:T(8,128)(2,1)} %collective-permute-done.5, bf16[6,12,128,128]{3,2,1,0:T(8,128)(2,1)} %all-gather.2.cloned.1.call-done, bf16[6,12,128,128]{3,2,1,0:T(8,128)(2,1)S(1)} %collective-permute-done.4), kind=kLoop, calls=%fused_computation.37 | loop fusion | flops 7077888 | bytes 14155776 | tf_op jit(solution)/shard_map/concatenate | solution.py:18
  123.9 50.9 %while.10 = (s32[]{:T(128)}, f32[6,12,128,128]{2,3,0,1:T(8,128)}, s32[6,3]{1,0:T(8,128)S(1)}, s32[18,12]{1,0:T(8,128)S(1)}, s32[6,12]{1,0:T(8,128)}, /*index=5*/...) while((s32[]{:T(128)}, f32[6,12,128,128]{2,3,0,1:T(8,128)}, ...), condition=%wide.region_1.2_spmd, body=%wide.region_0.1_spmd.sunk | while | flops 166333216 | bytes 9541871 | solution.py:71
  124.0 0.6 gather_fusion.1
  124.6 3.8 %gather_fusion = bf16[3,12,128,128]{3,2,1,0:T(8,128)(2,1)S(1)} fusion(bf16[18,12,128,128]{3,2,1,0:T(8,128)(2,1)} %get-tuple-element.178, s32[1024]{0:T(1024)S(1)} %pad_clamp_fusion.2), kind=kCustom, calls=%fused_computation.2.clone.1 | custom fusion | bytes 2359308 | tf_op jit(solution)/shard_map/while/body/eval_jaxpr/jit(_take)/gather | solution.py:25
  128.6 0.6 gather_fusion.2
  129.3 0.7 fusion.31
  130.0 0.9 convolution_convert_fusion.2
  131.0 1.5 fusion.32
  132.5 0.6 gather_fusion.1
  133.1 3.8 %gather_fusion = bf16[3,12,128,128]{3,2,1,0:T(8,128)(2,1)S(1)} fusion(bf16[18,12,128,128]{3,2,1,0:T(8,128)(2,1)} %get-tuple-element.178, s32[1024]{0:T(1024)S(1)} %pad_clamp_fusion.2), kind=kCustom, calls=%fused_computation.2.clone.1 | custom fusion | bytes 2359308 | tf_op jit(solution)/shard_map/while/body/eval_jaxpr/jit(_take)/gather | solution.py:25
  137.1 0.6 gather_fusion.2
  137.8 0.7 fusion.31
  138.5 0.9 convolution_convert_fusion.2
  139.4 1.5 fusion.32
  140.9 0.6 gather_fusion.1
  141.6 3.8 %gather_fusion = bf16[3,12,128,128]{3,2,1,0:T(8,128)(2,1)S(1)} fusion(bf16[18,12,128,128]{3,2,1,0:T(8,128)(2,1)} %get-tuple-element.178, s32[1024]{0:T(1024)S(1)} %pad_clamp_fusion.2), kind=kCustom, calls=%fused_computation.2.clone.1 | custom fusion | bytes 2359308 | tf_op jit(solution)/shard_map/while/body/eval_jaxpr/jit(_take)/gather | solution.py:25
  145.6 0.6 gather_fusion.2
  146.3 0.7 fusion.31
  147.0 0.9 convolution_convert_fusion.2
  147.9 1.5 fusion.32
  149.4 0.6 gather_fusion.1
  150.1 3.8 %gather_fusion = bf16[3,12,128,128]{3,2,1,0:T(8,128)(2,1)S(1)} fusion(bf16[18,12,128,128]{3,2,1,0:T(8,128)(2,1)} %get-tuple-element.178, s32[1024]{0:T(1024)S(1)} %pad_clamp_fusion.2), kind=kCustom, calls=%fused_computation.2.clone.1 | custom fusion | bytes 2359308 | tf_op jit(solution)/shard_map/while/body/eval_jaxpr/jit(_take)/gather | solution.py:25
  154.1 0.6 gather_fusion.2
  154.8 0.7 fusion.31
  155.5 0.9 convolution_convert_fusion.2
  156.4 1.5 fusion.32
  157.9 0.6 gather_fusion.1
  158.5 3.8 %gather_fusion = bf16[3,12,128,128]{3,2,1,0:T(8,128)(2,1)S(1)} fusion(bf16[18,12,128,128]{3,2,1,0:T(8,128)(2,1)} %get-tuple-element.178, s32[1024]{0:T(1024)S(1)} %pad_clamp_fusion.2), kind=kCustom, calls=%fused_computation.2.clone.1 | custom fusion | bytes 2359308 | tf_op jit(solution)/shard_map/while/body/eval_jaxpr/jit(_take)/gather | solution.py:25
  162.5 0.6 gather_fusion.2
  163.2 0.7 fusion.31
  163.9 0.9 convolution_convert_fusion.2
  164.9 1.5 fusion.32
  166.3 0.6 gather_fusion.1
  167.0 3.8 %gather_fusion = bf16[3,12,128,128]{3,2,1,0:T(8,128)(2,1)S(1)} fusion(bf16[18,12,128,128]{3,2,1,0:T(8,128)(2,1)} %get-tuple-element.178, s32[1024]{0:T(1024)S(1)} %pad_clamp_fusion.2), kind=kCustom, calls=%fused_computation.2.clone.1 | custom fusion | bytes 2359308 | tf_op jit(solution)/shard_map/while/body/eval_jaxpr/jit(_take)/gather | solution.py:25
  171.0 0.6 gather_fusion.2
  171.7 0.7 fusion.31
  172.4 0.9 convolution_convert_fusion.2
  173.3 1.5 fusion.32
  174.8 5.0 %all-to-all-start = ((f32[1,6,12,128,128]{3,4,1,0,2:T(8,128)}), f32[1,6,12,128,128]{3,4,1,0,2:T(8,128)}, u32[]{:S(2)}, u32[]{:S(2)}) async-start(f32[1,6,12,128,128]{3,4,1,0,2:T(8,128)} %bitcast.60), calls=%async_computation | async-start | bytes 9437184 | tf_op jit(solution)/shard_map/all_to_all | solution.py:72
  179.9 3.3 copy.13
  183.2 6.5 %bitcast_convert_fusion = f32[6,128,128]{0,2,1:T(8,128)} fusion(bf16[6,1,128,128]{0,3,2,1:T(8,128)(2,1)} %copy.13), kind=kLoop, calls=%fused_computation.38 | loop fusion | flops 98304 | bytes 589824 | tf_op jit(solution)/shard_map/convert_element_type | solution.py:76
  189.7 1.8 gather_fusion.3
  191.4 0.6 reduce_sum.28
  192.7 40.7 %all-to-all-done = f32[1,6,12,128,128]{3,4,1,0,2:T(8,128)} async-done(((f32[1,6,12,128,128]{3,4,1,0,2:T(8,128)}), f32[1,6,12,128,128]{3,4,1,0,2:T(8,128)}, u32[]{:S(2)}, u32[]{:S(2)}) %all-to-all-start) | async-done | bytes 4718624 | tf_op jit(solution)/shard_map/all_to_all | solution.py:72
  233.4 2.9 reduce_sum.27
  236.4 7.6 %copy.21 = f32[6,1,128,128]{0,3,2,1:T(8,128)} copy(f32[6,1,128,128]{2,3,1,0:T(8,128)S(1)} %copy.33) | data formatting | bytes 786432
  244.0 1.8 gather_fusion.4
  245.8 0.6 reduce_sum.29
  247.2 99.0 %psum.7 = f32[2]{0:T(128)} all-reduce(f32[2]{0:T(128)S(1)} %pad_maximum_fusion.1), channel_id=1, replica_groups=mesh['row'=16,'col'=8,'fib'=4] {'row','col','fib'}, use_global_device_ids=true, to_apply=%region_5.6 | all-reduce | flops 2 | bytes 16 | tf_op jit(solution)/shard_map/psum | solution.py:79
  346.3 1.1 copy.15
  (65 shorter events, 2.7 us)
Async XLA Ops:
  7.2 46.5 %all-gather.2.cloned.1.call-start = ((), (), s32[]{:S(2)}) async-start(), calls=%async_computation.1 | async-start | bytes 2949120 | tf_op jit(solution)/shard_map/all_gather | solution.py:43
  53.7 64.4 %collective-permute-start.4 = (bf16[6,12,128,128]{3,2,1,0:T(8,128)(2,1)}, bf16[6,12,128,128]{3,2,1,0:T(8,128)(2,1)S(1)}, u32[]{:S(2)}, u32[]{:S(2)}) collective-permute-start(bf16[6,12,128,128]{3,2,1,0:T(8,128)(2,1)} %all-gather.2.cloned.1.call-done), channel_id=1, source_target_pairs={{0,4},{4,8},{8,12},{12,16},{16,20},{20,24},{24,28},{28,32},{32,36}... | collective-permute-start | bytes 7077896 | tf_op jit(solution)/shard_map/ppermute | solution.py:16
  57.0 61.1 %collective-permute-start.5 = (bf16[6,12,128,128]{3,2,1,0:T(8,128)(2,1)}, bf16[6,12,128,128]{3,2,1,0:T(8,128)(2,1)}, u32[]{:S(2)}, u32[]{:S(2)}) collective-permute-start(bf16[6,12,128,128]{3,2,1,0:T(8,128)(2,1)} %all-gather.2.cloned.1.call-done), channel_id=1, source_target_pairs={{4,0},{8,4},{12,8},{16,12},{20,16},{24,20},{28,24},{32,28},{36,32}... | collective-permute-start | bytes 7077896 | tf_op jit(solution)/shard_map/ppermute | solution.py:17
  61.9 55.4 %collective-permute-start = (s32[6,12]{1,0:T(8,128)}, s32[6,12]{1,0:T(8,128)S(1)}, u32[]{:S(2)}, u32[]{:S(2)}) collective-permute-start(s32[6,12]{1,0:T(8,128)} %param.6), channel_id=1, source_target_pairs={{0,4},{4,8},{8,12},{12,16},{16,20},{20,24},{24,28},{28,32},{32,36}... | collective-permute-start | bytes 872 | tf_op jit(solution)/shard_map/ppermute | solution.py:16
  63.8 53.5 %collective-permute-start.1 = (s32[6,12]{1,0:T(8,128)}, s32[6,12]{1,0:T(8,128)S(1)}, u32[]{:S(2)}, u32[]{:S(2)}) collective-permute-start(s32[6,12]{1,0:T(8,128)} %param.6), channel_id=1, source_target_pairs={{4,0},{8,4},{12,8},{16,12},{20,16},{24,20},{28,24},{32,28},{36,32}... | collective-permute-start | bytes 872 | tf_op jit(solution)/shard_map/ppermute | solution.py:17
  68.7 43.5 %collective-permute-start.2 = (s32[6]{0:T(128)}, s32[6]{0:T(128)S(1)}, u32[]{:S(2)}, u32[]{:S(2)}) collective-permute-start(s32[6]{0:T(128)} %param.7), channel_id=1, source_target_pairs={{0,4},{4,8},{8,12},{12,16},{16,20},{20,24},{24,28},{28,32},{32,36}... | collective-permute-start | bytes 80 | tf_op jit(solution)/shard_map/ppermute | solution.py:16
  112.2 4.4 %collective-permute-start.3 = (s32[6]{0:T(128)}, s32[6]{0:T(128)S(1)}, u32[]{:S(2)}, u32[]{:S(2)}) collective-permute-start(s32[6]{0:T(128)} %param.7), channel_id=1, source_target_pairs={{4,0},{8,4},{12,8},{16,12},{20,16},{24,20},{28,24},{32,28},{36,32}... | collective-permute-start | bytes 80 | tf_op jit(solution)/shard_map/ppermute | solution.py:17
  118.0 5.9 %copy-start = (bf16[6,3,128,128]{3,2,1,0:T(8,128)(2,1)S(1)}, bf16[6,3,128,128]{3,2,1,0:T(8,128)(2,1)}, u32[]{:S(2)}) copy-start(bf16[6,3,128,128]{3,2,1,0:T(8,128)(2,1)} %param.5) | copy-start | bytes 1769476
  174.8 58.6 %all-to-all-start = ((f32[1,6,12,128,128]{3,4,1,0,2:T(8,128)}), f32[1,6,12,128,128]{3,4,1,0,2:T(8,128)}, u32[]{:S(2)}, u32[]{:S(2)}) async-start(f32[1,6,12,128,128]{3,4,1,0,2:T(8,128)} %bitcast.60), calls=%async_computation | async-start | bytes 9437184 | tf_op jit(solution)/shard_map/all_to_all | solution.py:72
Sparse Core Ops, SparseCore 0:
  10.1 43.5 all-gather.1
where the time goes:
time: 355 us; the launch traced here: 354 us
  waiting for transfers between devices  129 us (36%)
  blocking collectives  99 us (28%)
  local copies, waits for them, and re-layouts  50 us (14%)
  starting transfers between devices  24.9 us (7%)
  other arithmetic  21.6 us (6%)
  between operations  15.5 us (4%)
  matrix products  14.4 us (4%)
    psum x1, blocking collectives, body(): lax.psum(jnp.stack([trace_values, trace_square]), ('row', 'col', 'fib'))  99 us
    all_gather x1, waiting for transfers between devices, body(): full_rows = lax.all_gather(values, 'fib', axis=1, tiled=True)  45.8 us
    all_to_all x1, waiting for transfers between devices, body(): lax.all_to_all(partial_value[None], 'fib', split_axis=2, concat_axis=0, t...  40.7 us
    ppermute x3, waiting for transfers between devices, padded(): before = lax.ppermute(last, axis, up)  39.8 us
    gather x6, local copies, waits for them, and re-layouts, band_product(): picked = jnp.take(window, fetch_index, axis=0)  22.7 us
    ppermute x3, starting transfers between devices, padded(): after = lax.ppermute(initial, axis, down)  12.7 us
    dot_general x6, matrix products, band_product(): jnp.einsum('axy,ajyz->jxz', left_tiles, chosen, preferred_element_type=jn...  8.83 us
    unnamed x6, local copies, waits for them, and re-layouts  8.81 us
  transfers between devices with their start and end apart: 8, of which 4 were waited for; matrix products, arithmetic and copies ran while one was open for 4% of the time, Pallas kernels for 0%

commit v1 on v0

--- a/solution.py
+++ b/solution.py
@@ -4,6 +4,27 @@
 from jax.sharding import PartitionSpec as P
 
 BAND = 6
+
+
+def gather_around(shard, axis, dim):
+    count, index, width = (lax.axis_size(axis), lax.axis_index(axis), shard.shape[dim])
+    right = [(i, (i + 1) % count) for i in range(count)]
+    behind = [(i, (i - 1) % count) for i in range(count)]
+    out = jnp.zeros((*shard.shape[:dim], count * width, *shard.shape[dim + 1 :]), shard.dtype)
+    out = lax.dynamic_update_slice_in_dim(out, shard, index * width, axis=dim)
+    from_left = from_right = shard
+    half = count // 2
+    for step in range(1, half + 1):
+        from_left = lax.ppermute(from_left, axis, right)
+        out = lax.dynamic_update_slice_in_dim(
+            out, from_left, (index - step) % count * width, axis=dim
+        )
+        if step < count - half:
+            from_right = lax.ppermute(from_right, axis, behind)
+            out = lax.dynamic_update_slice_in_dim(
+                out, from_right, (index + step) % count * width, axis=dim
+            )
+    return out
 
 
 def padded(array, sides, width):
@@ -40,7 +61,7 @@
     slot_count = columns.shape[1]
     block_total = rows_here * lax.axis_size(("row", "col"))
     fib_index = lax.axis_index("fib")
-    full_rows = lax.all_gather(values, "fib", axis=1, tiled=True)
+    full_rows = gather_around(values, "fib", 1)
     window, window_cols, window_counts = (
         padded(full_rows, ((("row", "col"), 0),), BAND),
         padded(columns, ((("row", "col"), 0),), BAND),

time: 355 us -> 328 us (0.924)
  waiting for transfers between devices: 129 us -> 101 us
  starting transfers between devices: 24.9 us -> 47.2 us
  between operations: 15.5 us -> 2.27 us
  blocking collectives: 99 us -> 94.9 us
    all_gather x1 -> x0, waiting for transfers between devices: 45.8 us -> none  [body(): full_rows = lax.all_gather(values, 'fib', axis=1, tiled=True)]
    ppermute x0 -> x3, waiting for transfers between devices: none -> 16.3 us  [the longest x2 16.3 us: gather_around(): from_left = lax.ppermute(from_left, axis, right)]
    ppermute x0 -> x3, starting transfers between devices: none -> 13.9 us  [the longest x2 10.7 us: gather_around(): from_left = lax.ppermute(from_left, axis, right)]
    ppermute x3, starting transfers between devices: 12.7 us -> 17.6 us  [padded(): after = lax.ppermute(initial, axis, down)]
    eq x6, local copies, waits for them, and re-layouts: 4.19 us -> 0.06 us  [band_product(): picked_cols[:, None, :] == target_cols[None, :, None]]
    psum x1, blocking collectives: 99 us -> 94.9 us  [body(): lax.psum(jnp.stack([trace_values, trace_square]), ('row', 'col', 'fib'))]
    unnamed x6 -> x10, local copies, waits for them, and re-layouts: 8.81 us -> 8.85 us
  transfers between devices with their start and end apart: 8 -> 10, of which waited for: 4 -> 5; matrix products, arithmetic and copies ran while one was open for 4% -> 4% of each run, Pallas kernels for 0% -> 0%
where the time goes in v1:
time: 328 us; the launch traced here: 327 us
  waiting for transfers between devices  101 us (31%)
  blocking collectives  94.9 us (29%)
  local copies, waits for them, and re-layouts  48.9 us (15%)
  starting transfers between devices  47.2 us (14%)
  other arithmetic  18.9 us (6%)
  matrix products  14.5 us (4%)
    psum x1, blocking collectives, body(): lax.psum(jnp.stack([trace_values, trace_square]), ('row', 'col', 'fib'))  94.9 us
    ppermute x3, waiting for transfers between devices, padded(): before = lax.ppermute(last, axis, up)  41 us
    all_to_all x1, waiting for transfers between devices, body(): lax.all_to_all(partial_value[None], 'fib', split_axis=2, concat_axis=0, t...  40.9 us
    gather x6, local copies, waits for them, and re-layouts, band_product(): picked = jnp.take(window, fetch_index, axis=0)  22.7 us
    ppermute x3, starting transfers between devices, padded(): after = lax.ppermute(initial, axis, down)  17.6 us
    ppermute x2, waiting for transfers between devices, gather_around(): from_left = lax.ppermute(from_left, axis, right)  16.3 us
    ppermute x2, starting transfers between devices, gather_around(): from_left = lax.ppermute(from_left, axis, right)  10.7 us
    ppermute x3, starting transfers between devices, padded(): before = lax.ppermute(last, axis, up)  10.6 us
  transfers between devices with their start and end apart: 10, of which 5 were waited for; matrix products, arithmetic and copies ran while one was open for 4% of the time, Pallas kernels for 0%

profile of v1, /device:TPU:1, one launch (start us, length us, event | category | flops | bytes accessed | tf_op | source)
XLA Modules:
  0.0 327.5 jit_solution(2972432660495729232)
XLA Ops:
  0.6 4.1 %collective-permute-start.4 = (bf16[6,3,128,128]{3,2,1,0:T(8,128)(2,1)}, bf16[6,3,128,128]{3,2,1,0:T(8,128)(2,1)S(1)}, u32[]{:S(2)}, u32[]{:S(2)}) collective-permute-start(bf16[6,3,128,128]{3,2,1,0:T(8,128)(2,1)} %param.5), channel_id=1, source_target_pairs={{0,1},{1,2},{2,3},{3,0},{4,5},{5,6},{6,7},{7,4},{8,9},{9,10},{10,1... | collective-permute-start | bytes 1769480 | tf_op jit(solution)/shard_map/ppermute | solution.py:18
  4.7 3.2 collective-permute-start.5
  7.9 5.5 %collective-permute-done.4 = bf16[6,3,128,128]{3,2,1,0:T(8,128)(2,1)S(1)} collective-permute-done((bf16[6,3,128,128]{3,2,1,0:T(8,128)(2,1)}, bf16[6,3,128,128]{3,2,1,0:T(8,128)(2,1)S(1)}, u32[]{:S(2)}, u32[]{:S(2)}) %collective-permute-start.4) | collective-permute-done | bytes 589856 | tf_op jit(solution)/shard_map/ppermute | solution.py:18
  13.5 6.7 %collective-permute-start.6 = (bf16[6,3,128,128]{3,2,1,0:T(8,128)(2,1)S(1)}, bf16[6,3,128,128]{3,2,1,0:T(8,128)(2,1)}, u32[]{:S(2)}, u32[]{:S(2)}) collective-permute-start(bf16[6,3,128,128]{3,2,1,0:T(8,128)(2,1)S(1)} %collective-permute-done.4), channel_id=1, source_target_pairs={{0,1},{1,2},{2,3},{3,0},{4,5},{5,6},{6,7},{7,4},{8,9},{9,10},{10,1... | collective-permute-start | bytes 1769480 | tf_op jit(solution)/shard_map/ppermute | solution.py:18
  20.2 0.6 broadcast_in_dim.52
  21.0 1.2 constant_dynamic-update-slice_fusion.1
  22.2 10.8 %collective-permute-done.6 = bf16[6,3,128,128]{3,2,1,0:T(8,128)(2,1)} collective-permute-done((bf16[6,3,128,128]{3,2,1,0:T(8,128)(2,1)S(1)}, bf16[6,3,128,128]{3,2,1,0:T(8,128)(2,1)}, u32[]{:S(2)}, u32[]{:S(2)}) %collective-permute-start.6) | collective-permute-done | bytes 589856 | tf_op jit(solution)/shard_map/ppermute | solution.py:18
  32.9 1.1 constant_dynamic-update-slice_fusion
  34.1 6.7 %collective-permute-start.7 = (bf16[6,12,128,128]{3,2,1,0:T(8,128)(2,1)S(1)}, bf16[6,12,128,128]{3,2,1,0:T(8,128)(2,1)}, u32[]{:S(2)}, u32[]{:S(2)}) collective-permute-start(bf16[6,12,128,128]{3,2,1,0:T(8,128)(2,1)S(1)} %constant_dynamic-update-slice_fusion), channel_id=1, source_target_pairs={{0,4},{4,8},{8,12},{12,16},{16,20},{20,24},{24,28},{28,32},{32,36}... | collective-permute-start | bytes 7077896 | tf_op jit(solution)/shard_map/ppermute | solution.py:37
  40.8 10.9 %collective-permute-start.8 = (bf16[6,12,128,128]{3,2,1,0:T(8,128)(2,1)S(1)}, bf16[6,12,128,128]{3,2,1,0:T(8,128)(2,1)}, u32[]{:S(2)}, u32[]{:S(2)}) collective-permute-start(bf16[6,12,128,128]{3,2,1,0:T(8,128)(2,1)S(1)} %constant_dynamic-update-slice_fusion), channel_id=1, source_target_pairs={{4,0},{8,4},{12,8},{16,12},{20,16},{24,20},{28,24},{32,28},{36,32}... | collective-permute-start | bytes 7077896 | tf_op jit(solution)/shard_map/ppermute | solution.py:38
  51.7 1.9 collective-permute-start
  53.6 4.9 %collective-permute-start.1 = (s32[6,12]{1,0:T(8,128)S(1)}, s32[6,12]{1,0:T(8,128)S(1)}, u32[]{:S(2)}, u32[]{:S(2)}) collective-permute-start(s32[6,12]{1,0:T(8,128)S(1)} %copy-done.1), channel_id=1, source_target_pairs={{4,0},{8,4},{12,8},{16,12},{20,16},{24,20},{28,24},{32,28},{36,32}... | collective-permute-start | bytes 872 | tf_op jit(solution)/shard_map/ppermute | solution.py:38
  58.5 1.9 collective-permute-start.2
  60.8 41.0 %collective-permute-done.2 = s32[6]{0:T(128)S(1)} collective-permute-done((s32[6]{0:T(128)S(1)}, s32[6]{0:T(128)S(1)}, u32[]{:S(2)}, u32[]{:S(2)}) %collective-permute-start.2) | collective-permute-done | bytes 56 | tf_op jit(solution)/shard_map/ppermute | solution.py:37
  101.8 1.9 collective-permute-start.3
  103.7 2.4 collective-permute-done.3
  106.2 5.9 %pad_maximum_fusion = bf16[18,12,128,128]{3,2,1,0:T(8,128)(2,1)} fusion(bf16[6,12,128,128]{3,2,1,0:T(8,128)(2,1)} %collective-permute-done.8, bf16[6,12,128,128]{3,2,1,0:T(8,128)(2,1)S(1)} %constant_dynamic-update-slice_fusion, bf16[6,12,128,128]{3,2,1,0:T(8,128)(2,1)} %collective-permute-done.7), kind=kLoop, calls=%fused_computation.37 | loop fusion | flops 7077888 | bytes 14155776 | tf_op jit(solution)/shard_map/concatenate | solution.py:39
  112.1 46.9 %while.10 = (s32[]{:T(128)}, f32[6,12,128,128]{2,3,0,1:T(8,128)}, s32[6,3]{1,0:T(8,128)S(1)}, s32[18,12]{1,0:T(8,128)S(1)}, s32[6,12]{1,0:T(8,128)S(1)}, /*index...) while((s32[]{:T(128)}, f32[6,12,128,128]{2,3,0,1:T(8,128)}, ...), condition=%wide.region_1.2_spmd, body=%wide.region_0.1_spmd.sunk | while | flops 166333216 | bytes 9541871 | solution.py:92
  112.1 0.6 gather_fusion.1
  112.7 3.8 %gather_fusion = bf16[3,12,128,128]{3,2,1,0:T(8,128)(2,1)S(1)} fusion(bf16[18,12,128,128]{3,2,1,0:T(8,128)(2,1)} %get-tuple-element.178, s32[1024]{0:T(1024)S(1)} %pad_clamp_fusion.2), kind=kCustom, calls=%fused_computation.2.clone.1 | custom fusion | bytes 2359308 | tf_op jit(solution)/shard_map/while/body/eval_jaxpr/jit(_take)/gather | solution.py:46
  116.5 0.2 broadcast_select_fusion.7
  116.7 0.6 gather_fusion.2
  117.5 0.9 convolution_convert_fusion.2
  118.4 1.5 fusion.32
  119.9 0.6 gather_fusion.1
  120.6 3.8 %gather_fusion = bf16[3,12,128,128]{3,2,1,0:T(8,128)(2,1)S(1)} fusion(bf16[18,12,128,128]{3,2,1,0:T(8,128)(2,1)} %get-tuple-element.178, s32[1024]{0:T(1024)S(1)} %pad_clamp_fusion.2), kind=kCustom, calls=%fused_computation.2.clone.1 | custom fusion | bytes 2359308 | tf_op jit(solution)/shard_map/while/body/eval_jaxpr/jit(_take)/gather | solution.py:46
  124.4 0.2 broadcast_select_fusion.7
  124.6 0.6 gather_fusion.2
  125.3 0.9 convolution_convert_fusion.2
  126.2 1.5 fusion.32
  127.7 0.6 gather_fusion.1
  128.4 3.8 %gather_fusion = bf16[3,12,128,128]{3,2,1,0:T(8,128)(2,1)S(1)} fusion(bf16[18,12,128,128]{3,2,1,0:T(8,128)(2,1)} %get-tuple-element.178, s32[1024]{0:T(1024)S(1)} %pad_clamp_fusion.2), kind=kCustom, calls=%fused_computation.2.clone.1 | custom fusion | bytes 2359308 | tf_op jit(solution)/shard_map/while/body/eval_jaxpr/jit(_take)/gather | solution.py:46
  132.2 0.2 broadcast_select_fusion.7
  132.3 0.6 gather_fusion.2
  133.1 0.9 convolution_convert_fusion.2
  134.0 1.5 fusion.32
  135.5 0.6 gather_fusion.1
  136.2 3.8 %gather_fusion = bf16[3,12,128,128]{3,2,1,0:T(8,128)(2,1)S(1)} fusion(bf16[18,12,128,128]{3,2,1,0:T(8,128)(2,1)} %get-tuple-element.178, s32[1024]{0:T(1024)S(1)} %pad_clamp_fusion.2), kind=kCustom, calls=%fused_computation.2.clone.1 | custom fusion | bytes 2359308 | tf_op jit(solution)/shard_map/while/body/eval_jaxpr/jit(_take)/gather | solution.py:46
  140.2 0.6 gather_fusion.2
  140.9 0.9 convolution_convert_fusion.2
  141.8 1.5 fusion.32
  143.3 0.6 gather_fusion.1
  144.0 3.8 %gather_fusion = bf16[3,12,128,128]{3,2,1,0:T(8,128)(2,1)S(1)} fusion(bf16[18,12,128,128]{3,2,1,0:T(8,128)(2,1)} %get-tuple-element.178, s32[1024]{0:T(1024)S(1)} %pad_clamp_fusion.2), kind=kCustom, calls=%fused_computation.2.clone.1 | custom fusion | bytes 2359308 | tf_op jit(solution)/shard_map/while/body/eval_jaxpr/jit(_take)/gather | solution.py:46
  147.9 0.6 gather_fusion.2
  148.7 0.9 convolution_convert_fusion.2
  149.6 1.5 fusion.32
  151.1 0.6 gather_fusion.1
  151.8 3.8 %gather_fusion = bf16[3,12,128,128]{3,2,1,0:T(8,128)(2,1)S(1)} fusion(bf16[18,12,128,128]{3,2,1,0:T(8,128)(2,1)} %get-tuple-element.178, s32[1024]{0:T(1024)S(1)} %pad_clamp_fusion.2), kind=kCustom, calls=%fused_computation.2.clone.1 | custom fusion | bytes 2359308 | tf_op jit(solution)/shard_map/while/body/eval_jaxpr/jit(_take)/gather | solution.py:46
  155.6 0.2 broadcast_select_fusion.7
  155.7 0.6 gather_fusion.2
  156.5 0.9 convolution_convert_fusion.2
  157.4 1.5 fusion.32
  158.9 5.0 %all-to-all-start = ((f32[1,6,12,128,128]{3,4,1,0,2:T(8,128)}), f32[1,6,12,128,128]{3,4,1,0,2:T(8,128)}, u32[]{:S(2)}, u32[]{:S(2)}) async-start(f32[1,6,12,128,128]{3,4,1,0,2:T(8,128)} %bitcast.60), calls=%async_computation | async-start | bytes 9437184 | tf_op jit(solution)/shard_map/all_to_all | solution.py:93
  164.0 3.3 %copy.13 = bf16[6,1,128,128]{0,3,2,1:T(8,128)(2,1)} copy(bf16[6,1,128,128]{3,2,1,0:T(8,128)(2,1)S(1)} %slice.6) | data formatting | bytes 393216 | tf_op jit(solution)/shard_map/slice | solution.py:97
  167.3 6.5 %bitcast_convert_fusion = f32[6,128,128]{0,2,1:T(8,128)} fusion(bf16[6,1,128,128]{0,3,2,1:T(8,128)(2,1)} %copy.13), kind=kLoop, calls=%fused_computation.38 | loop fusion | flops 98304 | bytes 589824 | tf_op jit(solution)/shard_map/convert_element_type | solution.py:97
  173.8 1.8 gather_fusion.3
  175.5 0.6 reduce_sum.28
  176.8 40.9 %all-to-all-done = f32[1,6,12,128,128]{3,4,1,0,2:T(8,128)} async-done(((f32[1,6,12,128,128]{3,4,1,0,2:T(8,128)}), f32[1,6,12,128,128]{3,4,1,0,2:T(8,128)}, u32[]{:S(2)}, u32[]{:S(2)}) %all-to-all-start) | async-done | bytes 4718624 | tf_op jit(solution)/shard_map/all_to_all | solution.py:93
  217.7 2.9 reduce_sum.27
  220.6 7.6 %copy.21 = f32[6,1,128,128]{0,3,2,1:T(8,128)} copy(f32[6,1,128,128]{2,3,1,0:T(8,128)S(1)} %copy.33) | data formatting | bytes 786432
  228.3 1.8 gather_fusion.4
  230.0 0.6 reduce_sum.29
  231.5 94.9 %psum.7 = f32[2]{0:T(128)} all-reduce(f32[2]{0:T(128)S(1)} %pad_maximum_fusion.1), channel_id=1, replica_groups=mesh['row'=16,'col'=8,'fib'=4] {'row','col','fib'}, use_global_device_ids=true, to_apply=%region_5.6 | all-reduce | flops 2 | bytes 16 | tf_op jit(solution)/shard_map/psum | solution.py:100
  326.4 1.1 copy.15
  (77 shorter events, 2.4 us)
Async XLA Ops:
  0.6 20.1 %copy-start = (bf16[6,3,128,128]{3,2,1,0:T(8,128)(2,1)S(1)}, bf16[6,3,128,128]{3,2,1,0:T(8,128)(2,1)}, u32[]{:S(2)}) copy-start(bf16[6,3,128,128]{3,2,1,0:T(8,128)(2,1)} %param.5) | copy-start | bytes 1769476
  0.6 12.8 %collective-permute-start.4 = (bf16[6,3,128,128]{3,2,1,0:T(8,128)(2,1)}, bf16[6,3,128,128]{3,2,1,0:T(8,128)(2,1)S(1)}, u32[]{:S(2)}, u32[]{:S(2)}) collective-permute-start(bf16[6,3,128,128]{3,2,1,0:T(8,128)(2,1)} %param.5), channel_id=1, source_target_pairs={{0,1},{1,2},{2,3},{3,0},{4,5},{5,6},{6,7},{7,4},{8,9},{9,10},{10,1... | collective-permute-start | bytes 1769480 | tf_op jit(solution)/shard_map/ppermute | solution.py:18
  4.7 16.3 %collective-permute-start.5 = (bf16[6,3,128,128]{3,2,1,0:T(8,128)(2,1)}, bf16[6,3,128,128]{3,2,1,0:T(8,128)(2,1)}, u32[]{:S(2)}, u32[]{:S(2)}) collective-permute-start(bf16[6,3,128,128]{3,2,1,0:T(8,128)(2,1)} %param.5), channel_id=1, source_target_pairs={{0,3},{1,0},{2,1},{3,2},{4,7},{5,4},{6,5},{7,6},{8,11},{9,8},{10,9... | collective-permute-start | bytes 1769480 | tf_op jit(solution)/shard_map/ppermute | solution.py:23
  13.5 19.5 %collective-permute-start.6 = (bf16[6,3,128,128]{3,2,1,0:T(8,128)(2,1)S(1)}, bf16[6,3,128,128]{3,2,1,0:T(8,128)(2,1)}, u32[]{:S(2)}, u32[]{:S(2)}) collective-permute-start(bf16[6,3,128,128]{3,2,1,0:T(8,128)(2,1)S(1)} %collective-permute-done.4), channel_id=1, source_target_pairs={{0,1},{1,2},{2,3},{3,0},{4,5},{5,6},{6,7},{7,4},{8,9},{9,10},{10,1... | collective-permute-start | bytes 1769480 | tf_op jit(solution)/shard_map/ppermute | solution.py:18
  20.8 30.9 %copy-start.1 = (s32[6,12]{1,0:T(8,128)S(1)}, s32[6,12]{1,0:T(8,128)}, u32[]{:S(2)}) copy-start(s32[6,12]{1,0:T(8,128)} %param.6) | copy-start | bytes 868
  20.8 37.7 %copy-start.2 = (s32[6]{0:T(128)S(1)}, s32[6]{0:T(128)}, u32[]{:S(2)}) copy-start(s32[6]{0:T(128)} %param.7) | copy-start | bytes 76
  34.1 72.1 %collective-permute-start.7 = (bf16[6,12,128,128]{3,2,1,0:T(8,128)(2,1)S(1)}, bf16[6,12,128,128]{3,2,1,0:T(8,128)(2,1)}, u32[]{:S(2)}, u32[]{:S(2)}) collective-permute-start(bf16[6,12,128,128]{3,2,1,0:T(8,128)(2,1)S(1)} %constant_dynamic-update-slice_fusion), channel_id=1, source_target_pairs={{0,4},{4,8},{8,12},{12,16},{16,20},{20,24},{24,28},{28,32},{32,36}... | collective-permute-start | bytes 7077896 | tf_op jit(solution)/shard_map/ppermute | solution.py:37
  40.8 65.3 %collective-permute-start.8 = (bf16[6,12,128,128]{3,2,1,0:T(8,128)(2,1)S(1)}, bf16[6,12,128,128]{3,2,1,0:T(8,128)(2,1)}, u32[]{:S(2)}, u32[]{:S(2)}) collective-permute-start(bf16[6,12,128,128]{3,2,1,0:T(8,128)(2,1)S(1)} %constant_dynamic-update-slice_fusion), channel_id=1, source_target_pairs={{4,0},{8,4},{12,8},{16,12},{20,16},{24,20},{28,24},{32,28},{36,32}... | collective-permute-start | bytes 7077896 | tf_op jit(solution)/shard_map/ppermute | solution.py:38
  51.7 54.4 %collective-permute-start = (s32[6,12]{1,0:T(8,128)S(1)}, s32[6,12]{1,0:T(8,128)S(1)}, u32[]{:S(2)}, u32[]{:S(2)}) collective-permute-start(s32[6,12]{1,0:T(8,128)S(1)} %copy-done.1), channel_id=1, source_target_pairs={{0,4},{4,8},{8,12},{12,16},{16,20},{20,24},{24,28},{28,32},{32,36}... | collective-permute-start | bytes 872 | tf_op jit(solution)/shard_map/ppermute | solution.py:37
  53.6 52.5 %collective-permute-start.1 = (s32[6,12]{1,0:T(8,128)S(1)}, s32[6,12]{1,0:T(8,128)S(1)}, u32[]{:S(2)}, u32[]{:S(2)}) collective-permute-start(s32[6,12]{1,0:T(8,128)S(1)} %copy-done.1), channel_id=1, source_target_pairs={{4,0},{8,4},{12,8},{16,12},{20,16},{24,20},{28,24},{32,28},{36,32}... | collective-permute-start | bytes 872 | tf_op jit(solution)/shard_map/ppermute | solution.py:38
  58.5 43.2 %collective-permute-start.2 = (s32[6]{0:T(128)S(1)}, s32[6]{0:T(128)S(1)}, u32[]{:S(2)}, u32[]{:S(2)}) collective-permute-start(s32[6]{0:T(128)S(1)} %copy-done.2), channel_id=1, source_target_pairs={{0,4},{4,8},{8,12},{12,16},{16,20},{20,24},{24,28},{28,32},{32,36}... | collective-permute-start | bytes 80 | tf_op jit(solution)/shard_map/ppermute | solution.py:37
  101.8 4.3 %collective-permute-start.3 = (s32[6]{0:T(128)S(1)}, s32[6]{0:T(128)S(1)}, u32[]{:S(2)}, u32[]{:S(2)}) collective-permute-start(s32[6]{0:T(128)S(1)} %copy-done.2), channel_id=1, source_target_pairs={{4,0},{8,4},{12,8},{16,12},{20,16},{24,20},{28,24},{32,28},{36,32}... | collective-permute-start | bytes 80 | tf_op jit(solution)/shard_map/ppermute | solution.py:38
  158.9 58.8 %all-to-all-start = ((f32[1,6,12,128,128]{3,4,1,0,2:T(8,128)}), f32[1,6,12,128,128]{3,4,1,0,2:T(8,128)}, u32[]{:S(2)}, u32[]{:S(2)}) async-start(f32[1,6,12,128,128]{3,4,1,0,2:T(8,128)} %bitcast.60), calls=%async_computation | async-start | bytes 9437184 | tf_op jit(solution)/shard_map/all_to_all | solution.py:93
